TPU v7x, 32 devices: a whole 2x2x4 slice. The times are simulated.
32 devices in a mesh: groups: 2 (over y), state: 4 (over z), type: 4 (over x, core).
Axes of the slice: x: 2, y: 2, z: 4, core: 2. Of those that a mesh axis runs over, the one named last changes fastest.
Arguments:
- value_in: bfloat16 [16384, 2048], P(('groups', 'state'), 'type'), parts along dimension 0, may hold values from -7.5 to 7.5
- cotangent: bfloat16 [16384, 2048], P(('groups', 'state'), 'type'), parts along dimension 0, may hold values from -100 to 100
- state_util: float32 [2, 16384], P(None, ('groups', 'state')), parts along dimension 1, may hold values from -300 to 300
- taste: float32 [2, 4096], P(None, ('groups', 'type')), parts along dimension 1, may hold values from -6 to 6
- tiles: bfloat16 [128, 2, 6, 128, 128], P(('groups', 'state')), parts along dimension 0, may hold values from 0 to 0.0051879883
- dest_block: int32 [128, 2, 6], P(('groups', 'state')), parts along dimension 0, may hold values from 0 to 63, as said below
- counts: int32 [128, 2], P(('groups', 'state')), parts along dimension 0, may hold values from 1 to 6
Outputs:
- value_out: float32 [16384, 2048], P(('groups', 'state'), 'type'), parts along dimension 0
- adjoint: float32 [16384, 2048], P(('groups', 'state'), 'type'), parts along dimension 0
- grad_util: float32 [2, 16384], P(None, ('groups', 'state')), parts along dimension 1
- grad_taste: float32 [2, 4096], P(None, ('groups', 'type')), parts along dimension 1
There are 2 independent parts, one for each index of `groups`. A program takes and returns all parts, laid end to end along the dimension named above; each array names one. Nothing has to cross between parts.
Inputs may be any that keep to these rules, and one draw needn't show every extreme that they name: `dest_block`: entries at or beyond a list's count name blocks of the list's own run of 16 blocks. In each run of 16 blocks exactly 16 used entries name blocks outside the run, at most 6 of them in any one other run, and exactly 6 in some other run.
All inputs are finite; a program needn't handle non-finite values.
Results may differ from a plain program's by a relative error of at most 0.0012.
Values may be sent and summed in bfloat16 or wider, within the bound.
A program may use at most 192 MiB of HBM per device.

v0:
```python
import jax
import jax.numpy as jnp
from jax import lax
from jax.sharding import PartitionSpec as P


def local(value_in, cotangent, state_util, taste, tiles, dest_block, counts):
    block_count, action_count, entry_count, tile_rows, _ = tiles.shape
    type_width = value_in.shape[1]
    device_count = lax.axis_size("state")
    my_index = lax.axis_index("state")
    capacity = max(2, (block_count + device_count - 2) // (device_count - 1))
    entry_total = block_count * action_count * entry_count
    value_blocks = value_in.reshape(block_count, tile_rows, type_width)
    flat_dest = dest_block.reshape(entry_total)
    owner = flat_dest // block_count
    local_block = flat_dest % block_count
    used = (jnp.arange(entry_count, dtype=jnp.int32)[None, None, :] < counts[:, :, None]).reshape(
        entry_total
    )
    remote = used & (owner != my_index)
    local_used = used & (owner == my_index)
    peer_ids = jnp.arange(device_count, dtype=jnp.int32)
    owner_hits = (remote[:, None] & (owner[:, None] == peer_ids[None, :])).astype(jnp.int32)
    earlier = jnp.cumsum(owner_hits, axis=0) - owner_hits
    slot_of = jnp.sum(earlier * owner_hits, axis=1)
    target = jnp.where(remote, owner * capacity + slot_of, device_count * capacity)
    request = (
        jnp.full((device_count * capacity,), -1, jnp.int32).at[target].set(local_block, mode="drop")
    )
    source_entry = (
        jnp.full((device_count * capacity,), -1, jnp.int32)
        .at[target]
        .set(jnp.arange(entry_total, dtype=jnp.int32), mode="drop")
    )
    wanted = lax.all_to_all(
        request.reshape(device_count, capacity), "state", split_axis=0, concat_axis=0, tiled=True
    )
    outgoing = jnp.take(value_blocks, jnp.clip(wanted.reshape(-1), 0, block_count - 1), axis=0)
    incoming = lax.all_to_all(
        outgoing.reshape(device_count, capacity, tile_rows, type_width),
        "state",
        split_axis=0,
        concat_axis=0,
        tiled=True,
    )
    table = jnp.concatenate(
        [value_blocks, incoming.reshape(device_count * capacity, tile_rows, type_width)], axis=0
    )
    lookup = jnp.where(remote, block_count + target, local_block)
    picked = jnp.take(table, lookup, axis=0)
    picked = jnp.where(used[:, None, None], picked, jnp.zeros_like(picked))
    picked = picked.reshape(block_count, action_count, entry_count, tile_rows, type_width)
    cont = jnp.einsum("bamij,bamjk->baik", tiles, picked, preferred_element_type=jnp.float32)
    util_grid = state_util.reshape(action_count, block_count, tile_rows).transpose(1, 0, 2)[
        :, :, :, None
    ]
    scores = util_grid + taste[None, :, None, :] + 0.95 * cont
    largest = jnp.max(scores, axis=1)
    value = largest + jnp.log(jnp.sum(jnp.exp(scores - largest[:, None]), axis=1))
    prob = jnp.exp(scores - value[:, None])
    grad_q = cotangent.reshape(block_count, 1, tile_rows, type_width).astype(jnp.float32) * prob
    util_part = (
        jnp.sum(grad_q, axis=3).transpose(1, 0, 2).reshape(action_count, block_count * tile_rows)
    )
    util_total = lax.psum(util_part, "type") / (type_width * lax.axis_size("type"))
    taste_total = lax.psum(jnp.sum(grad_q, axis=(0, 2)), "state") / (
        block_count * tile_rows * device_count
    )
    scaled = (0.95 * grad_q).astype(jnp.bfloat16)
    slot_valid = source_entry >= 0
    safe_entry = jnp.clip(source_entry, 0, entry_total - 1)
    contrib = jnp.einsum(
        "bamij,baik->bamjk", tiles, scaled, preferred_element_type=jnp.float32
    ).reshape(entry_total, tile_rows, type_width)
    outbound = jnp.where(
        slot_valid[:, None, None], jnp.take(contrib, safe_entry, axis=0), 0.0
    ).astype(jnp.bfloat16)
    returned = lax.all_to_all(
        outbound.reshape(device_count, capacity, tile_rows, type_width),
        "state",
        split_axis=0,
        concat_axis=0,
        tiled=True,
    )
    block_ids = jnp.arange(block_count, dtype=jnp.int32)
    local_select = (local_used[:, None] & (local_block[:, None] == block_ids[None, :])).astype(
        jnp.float32
    )
    own_terms = jnp.einsum("rd,rjk->djk", local_select, contrib, precision=lax.Precision.HIGHEST)
    arrive_select = (wanted.reshape(-1)[None, :] == block_ids[:, None]).astype(jnp.bfloat16)
    arrived = jnp.dot(
        arrive_select,
        returned.reshape(device_count * capacity, tile_rows * type_width),
        preferred_element_type=jnp.float32,
    )
    adjoint = own_terms + arrived.reshape(block_count, tile_rows, type_width)
    value_out = value.reshape(block_count * tile_rows, type_width)
    return (
        value_out,
        adjoint.reshape(block_count * tile_rows, type_width),
        util_total,
        taste_total,
    )


def solution(mesh):
    return jax.shard_map(
        local,
        mesh=mesh,
        in_specs=(
            P(("groups", "state"), "type"),
            P(("groups", "state"), "type"),
            P(None, ("groups", "state")),
            P(None, ("groups", "type")),
            P(("groups", "state"), None, None, None, None),
            P(("groups", "state"), None, None),
            P(("groups", "state"), None),
        ),
        out_specs=(
            P(("groups", "state"), "type"),
            P(("groups", "state"), "type"),
            P(None, ("groups", "state")),
            P(None, ("groups", "type")),
        ),
        check_vma=False,
    )
```

profile of v0, /device:TPU:0, one launch (start us, length us, event | category | flops | bytes accessed | tf_op | source)
XLA Modules:
  0.0 337.9 jit_solution(11441029719686296648)
XLA Ops:
  0.6 0.8 copy.37
  1.4 0.1 iota_compare_fusion.1
  1.5 0.1 lt.106
  1.6 0.1 lt.109
  1.7 0.8 copy.38
  2.5 0.1 reshape.392
  2.6 0.1 reshape.396
  2.8 1.2 reduce-window.6
  4.0 0.1 slice.18
  4.1 0.1 copy.43
  4.3 0.1 copy.44
  4.4 0.1 add_bitcast_fusion
  4.5 1.2 scatter_custom_fusion
  5.7 0.1 all_to_all.12
  5.8 11.7 %all_to_all.19 = s32[4,1,6]{2,1,0:T(1,128)S(1)} all-to-all(s32[4,1,6]{2,1,0:T(1,128)S(1)} %bitcast.86), channel_id=1, replica_groups=mesh['groups'=2,'state'=4,'type'=4] {'state'}, dimensions={0} | all-to-all | bytes 192 | tf_op jit(solution)/shard_map/all_to_all | solution.py:36
  17.5 0.5 broadcast.505
  18.0 0.7 fusion.47
  18.7 0.1 min.24
  18.8 2.3 gather_fusion
  21.1 2.0 broadcast_select_fusion
  23.2 0.0 copy-start.1
  23.2 4.8 %all-to-all-start.1 = ((bf16[4,6,128,512]{3,2,1,0:T(8,128)(2,1)}), bf16[4,6,128,512]{3,2,1,0:T(8,128)(2,1)}, u32[]{:S(2)}, u32[]{:S(2)}) async-start(bf16[4,6,128,512]{3,2,1,0:T(8,128)(2,1)} %broadcast_select_fusion), calls=%async_computation.1 | async-start | bytes 6291456 | tf_op jit(solution)/shard_map/all_to_all | solution.py:40
  28.0 0.1 reduce_sum.41
  28.1 1.4 scatter_custom_fusion.1
  29.5 0.1 broadcast_in_dim.91
  29.6 0.1 broadcast_in_dim.89
  29.7 4.1 %copy.49 = f32[16,128,512]{1,2,0:T(8,128)} copy(bf16[16,128,512]{2,1,0:T(8,128)(2,1)} %bitcast.81) | data formatting | bytes 6291456 | tf_op jit(solution)/shard_map/convert_element_type | solution.py:62
  33.8 0.1 compare_and_fusion
  33.9 63.7 %all-to-all-done.1 = bf16[4,6,128,512]{3,2,1,0:T(8,128)(2,1)} async-done(((bf16[4,6,128,512]{3,2,1,0:T(8,128)(2,1)}), bf16[4,6,128,512]{3,2,1,0:T(8,128)(2,1)}, u32[]{:S(2)}, u32[]{:S(2)}) %all-to-all-start.1) | async-done | bytes 3145760 | tf_op jit(solution)/shard_map/all_to_all | solution.py:40
  97.5 0.0 copy-done.1
  97.5 4.7 %pad_maximum_fusion = bf16[40,128,512]{2,1,0:T(8,128)(2,1)} fusion(bf16[24,128,512]{2,1,0:T(8,128)(2,1)} %bitcast.11, bf16[16,128,512]{2,1,0:T(8,128)(2,1)S(1)} %bitcast.75), kind=kLoop, calls=%fused_computation.20 | loop fusion | flops 2621440 | bytes 10485760 | tf_op jit(solution)/shard_map/concatenate | solution.py:47
  102.3 13.6 %gather_fusion.1 = bf16[192,128,512]{2,1,0:T(8,128)(2,1)} fusion(bf16[40,128,512]{2,1,0:T(8,128)(2,1)} %pad_maximum_fusion, s32[1024]{0:T(1024)S(1)} %pad_clamp_fusion.1), kind=kCustom, calls=%fused_computation.1 | custom fusion | bytes 50332416 | tf_op jit(solution)/shard_map/jit(_take)/gather | solution.py:51
  115.8 0.0 copy-start.2
  115.8 0.0 copy-start.3
  115.8 32.6 %copy.47 = bf16[16,2,6,128,512]{3,4,2,1,0:T(8,128)(2,1)} copy(bf16[16,2,6,128,512]{4,3,2,1,0:T(8,128)(2,1)} %bitcast.73) | data formatting | bytes 50331648 | tf_op jit(solution)/shard_map/jit(_take)/gather | solution.py:51
  148.4 0.0 copy-done.2
  148.4 0.0 copy-done.3
  148.4 15.0 %fusion.48 = (f32[16,128,512]{1,2,0:T(8,128)}, f32[16,2,128,512]{2,3,1,0:T(8,128)S(1)}) fusion(bf16[16,2,6,128,128]{4,3,2,1,0:T(8,128)(2,1)} %param.11, bf16[16,2,6,128,512]{3,4,2,1,0:T(8,128)(2,1)} %copy.47, pred[16,2,6]{2,1,0:T(4,128)(4,1)S(1)} %compare_and_fusion, pred[16,2,6]{2,1,0:T(4,128)(4,1)S(1)} %iota_compare_fusion.1, ...), kind=kOutput, calls=%fused_computation.102 | convolution fusion | flops 3253731328 | bytes 44061056 | tf_op jit(solution)/shard_map/bamij,bamjk->baik/dot_general | solution.py:54
  163.4 0.0 copy-start
  163.4 9.7 %exponential_reduce_fusion = f32[16,128,512]{1,2,0:T(8,128)} fusion(f32[16,2,128,512]{2,3,1,0:T(8,128)S(1)} %get-tuple-element.17, f32[16,128,512]{1,2,0:T(8,128)} %get-tuple-element.16), kind=kLoop, calls=%fused_computation.16 | loop fusion | flops 3145728 | bytes 16777216 | tf_op jit(solution)/shard_map/reduce_sum | solution.py:60
  173.1 0.0 copy-done
  173.1 6.0 %log_add_fusion = f32[16,128,512]{1,2,0:T(8,128)} fusion(f32[16,128,512]{1,2,0:T(8,128)} %get-tuple-element.16, f32[16,128,512]{1,2,0:T(8,128)} %exponential_reduce_fusion), kind=kLoop, calls=%fused_computation.26 | loop fusion | flops 1048576 | bytes 12582912 | tf_op jit(solution)/shard_map/add | solution.py:60
  179.1 24.5 %fusion.10 = f32[16,2,512,6,128]{4,2,3,1,0:T(8,128)} fusion(bf16[16,2,6,128,128]{4,3,2,1,0:T(8,128)(2,1)} %param.11, f32[16,2,128,512]{2,3,1,0:T(8,128)} %copy-done, f32[16,128,512]{1,2,0:T(8,128)} %log_add_fusion, f32[16,128,512]{1,2,0:T(8,128)} %copy.49), kind=kOutput, calls=%fused_computation.22 | convolution fusion | flops 3229614080 | bytes 73400320 | tf_op jit(solution)/shard_map/bamij,baik->bamjk/dot_general | solution.py:73
  203.6 4.4 %gather_fusion.2 = bf16[24,128,512]{1,2,0:T(8,128)(2,1)S(1)} fusion(f32[192,128,512]{1,2,0:T(8,128)} %bitcast.71, s32[1024]{0:T(1024)S(1)} %pad_clamp_fusion), kind=kCustom, calls=%fused_computation.2 | custom fusion | bytes 6291552 | tf_op jit(solution)/shard_map/jit(_take)/gather | solution.py:77
  208.1 2.8 copy.51
  210.9 5.0 %select_convert_fusion = bf16[4,6,128,512]{3,2,1,0:T(8,128)(2,1)} fusion(bf16[4,6,128,512]{3,2,1,0:T(8,128)(2,1)} %bitcast.78, pred[4,6]{1,0:T(4,128)(4,1)S(1)} %broadcast_in_dim.91, pred[4,6]{1,0:T(4,128)(4,1)S(1)} %broadcast_in_dim.89), kind=kLoop, calls=%fused_computation.17 | loop fusion | flops 3145728 | bytes 6291504 | tf_op jit(solution)/shard_map/convert_element_type | solution.py:78
  215.8 3.7 %all-to-all-start.2 = ((bf16[4,6,128,512]{3,2,1,0:T(8,128)(2,1)}), bf16[4,6,128,512]{3,2,1,0:T(8,128)(2,1)S(1)}, u32[]{:S(2)}, u32[]{:S(2)}) async-start(bf16[4,6,128,512]{3,2,1,0:T(8,128)(2,1)} %select_convert_fusion), calls=%async_computation.2 | async-start | bytes 6291456 | tf_op jit(solution)/shard_map/all_to_all | solution.py:79
  219.5 0.1 reshape.399
  219.6 5.3 %copy.48 = f32[16,128,512]{2,1,0:T(8,128)} copy(f32[16,128,512]{1,2,0:T(8,128)} %log_add_fusion) | data formatting | bytes 8388608 | tf_op jit(solution)/shard_map/add | solution.py:60
  225.0 49.2 %copy.50 = f32[192,128,512]{2,0,1:T(8,128)} copy(f32[192,128,512]{1,2,0:T(8,128)} %bitcast.72) | data formatting | bytes 100663296 | tf_op jit(solution)/shard_map/reshape | solution.py:75
  274.2 7.5 %fusion.7 = (f32[2,512]{1,0:T(2,128)S(1)}, f32[16,2,128]{2,1,0:T(2,128)S(1)}) fusion(f32[16,2,128,512]{2,3,1,0:T(8,128)} %copy-done, f32[16,128,512]{1,2,0:T(8,128)} %log_add_fusion, f32[16,128,512]{1,2,0:T(8,128)} %copy.49), kind=kLoop, calls=%fused_computation.18 | loop fusion | flops 8383488 | bytes 16797696 | tf_op jit(solution)/shard_map/reduce_sum | solution.py:67
  281.7 12.2 %psum.15 = f32[2,512]{1,0:T(2,128)S(1)} all-reduce(f32[2,512]{1,0:T(2,128)S(1)} %get-tuple-element.4), channel_id=1, replica_groups=mesh['groups'=2,'state'=4,'type'=4] {'state'}, use_global_device_ids=true, to_apply=%region_10.11 | all-reduce | flops 1024 | bytes 8192 | tf_op jit(solution)/shard_map/psum | solution.py:67
  293.8 10.1 %psum.14 = f32[2,2048]{1,0:T(2,128)S(1)} all-reduce(f32[2,2048]{1,0:T(2,128)S(1)} %bitcast.82), channel_id=1, replica_groups=mesh['groups'=2,'state'=4,'type'=4] {'type'}, use_global_device_ids=true, to_apply=%region_8.9 | all-reduce | flops 4096 | bytes 32768 | tf_op jit(solution)/shard_map/psum | solution.py:66
  303.9 0.6 broadcast_multiply_fusion.1
  304.5 0.6 broadcast_multiply_fusion
  305.1 23.2 %fusion.26 = f32[16,128,512]{2,0,1:T(8,128)} fusion(f32[192,128,512]{2,0,1:T(8,128)} %copy.50, s32[192]{0:T(256)S(1)} %and_select_fusion.4, pred[192]{0:T(512)(128)(4,1)S(1)} %get-tuple-element.10), kind=kOutput, calls=%fused_computation.45 | convolution fusion | flops 2415925248 | bytes 54526912 | tf_op jit(solution)/shard_map/rd,rjk->djk/dot_general | solution.py:90
  328.4 0.0 all-to-all-done.2
  328.4 5.1 %fusion.20 = f32[16,128,512]{2,0,1:T(8,128)S(1)} fusion(f32[16,128,512]{2,0,1:T(8,128)} %fusion.26, s32[24]{0:T(128)S(1)} %reshape.399, bf16[3,8,128,512]{3,2,1,0:T(8,128)(2,1)S(1)} %bitcast.77), kind=kOutput, calls=%fused_computation.31 | convolution fusion | flops 51380608 | bytes 11534432 | tf_op jit(solution)/shard_map/dot_general | solution.py:92
  333.5 4.4 %copy.53 = f32[16,128,512]{2,1,0:T(8,128)} copy(f32[16,128,512]{2,0,1:T(8,128)S(1)} %fusion.20) | data formatting | bytes 8388608 | tf_op jit(solution)/shard_map/add | solution.py:97
  (19 shorter events, 0.2 us)
Async XLA Ops:
  23.2 74.4 %copy-start.1 = (bf16[2048,512]{1,0:T(8,128)(2,1)S(1)}, bf16[2048,512]{1,0:T(8,128)(2,1)}, u32[]{:S(2)}) copy-start(bf16[2048,512]{1,0:T(8,128)(2,1)} %param.7) | copy-start | bytes 6291460
  23.2 74.4 %all-to-all-start.1 = ((bf16[4,6,128,512]{3,2,1,0:T(8,128)(2,1)}), bf16[4,6,128,512]{3,2,1,0:T(8,128)(2,1)}, u32[]{:S(2)}, u32[]{:S(2)}) async-start(bf16[4,6,128,512]{3,2,1,0:T(8,128)(2,1)} %broadcast_select_fusion), calls=%async_computation.1 | async-start | bytes 6291456 | tf_op jit(solution)/shard_map/all_to_all | solution.py:40
  115.8 32.6 %copy-start.2 = (f32[2,2048]{1,0:T(2,128)S(1)}, f32[2,2048]{1,0:T(2,128)}, u32[]{:S(2)}) copy-start(f32[2,2048]{1,0:T(2,128)} %param.9) | copy-start | bytes 49156
  115.8 32.6 %copy-start.3 = (f32[2,512]{1,0:T(2,128)S(1)}, f32[2,512]{1,0:T(2,128)}, u32[]{:S(2)}) copy-start(f32[2,512]{1,0:T(2,128)} %param.10) | copy-start | bytes 12292
  163.4 9.7 %copy-start = (f32[16,2,128,512]{2,3,1,0:T(8,128)}, f32[16,2,128,512]{2,3,1,0:T(8,128)S(1)}, u32[]{:S(2)}) copy-start(f32[16,2,128,512]{2,3,1,0:T(8,128)S(1)} %get-tuple-element.17) | copy-start | bytes 25165828
  215.8 112.5 %all-to-all-start.2 = ((bf16[4,6,128,512]{3,2,1,0:T(8,128)(2,1)}), bf16[4,6,128,512]{3,2,1,0:T(8,128)(2,1)S(1)}, u32[]{:S(2)}, u32[]{:S(2)}) async-start(bf16[4,6,128,512]{3,2,1,0:T(8,128)(2,1)} %select_convert_fusion), calls=%async_computation.2 | async-start | bytes 6291456 | tf_op jit(solution)/shard_map/all_to_all | solution.py:79
where the time goes:
time: 340 us; the launch traced here: 338 us
  local copies, waits for them, and re-layouts  125 us (37%)
  matrix products  67.8 us (20%)
  waiting for transfers between devices  63.7 us (19%)
  other arithmetic  38.5 us (11%)
  blocking collectives  34 us (10%)
  starting transfers between devices  8.47 us (2%)
    all_to_all x1, waiting for transfers between devices, local(): lax.all_to_all(outgoing.reshape(device_count, capacity, tile_rows, type_w...  63.7 us
    reshape x1, local copies, waits for them, and re-layouts, local(): contrib = jnp.einsum('bamij,baik->bamjk', tiles, scaled, preferred_elemen...  49.2 us
    gather x2, local copies, waits for them, and re-layouts, local(): picked = jnp.take(table, lookup, axis=0)  46.1 us
    dot_general x1, matrix products, local(): jnp.einsum('bamij,baik->bamjk', tiles, scaled, preferred_element_type=jnp...  24.5 us
    dot_general x1, matrix products, local(): jnp.einsum('rd,rjk->djk', local_select, contrib, precision=lax.Precision....  23.2 us
    dot_general x1, matrix products, local(): jnp.einsum('bamij,bamjk->baik', tiles, picked, preferred_element_type=jnp...  15 us
    psum x1, blocking collectives, local(): lax.psum(jnp.sum(grad_q, axis=(0, 2)), 'state')  12.2 us
    all_to_all x1, blocking collectives, local(): lax.all_to_all(request.reshape(device_count, capacity), 'state', split_ax...  11.7 us
  transfers between devices with their start and end apart: 2, of which 1 were waited for; matrix products, arithmetic and copies ran while one was open for 27% of the time, Pallas kernels for 0%

commit v1 on v0

--- a/solution.py
+++ b/solution.py
@@ -2,6 +2,28 @@
 import jax.numpy as jnp
 from jax import lax
 from jax.sharding import PartitionSpec as P
+
+
+def cut_along(x, dim, size):
+    before, after = (x.shape[:dim], x.shape[dim + 1 :])
+    return jnp.moveaxis(x.reshape(*before, size, -1, *after), dim, 0)
+
+
+def joined_along(blocks, dim):
+    blocks = jnp.moveaxis(blocks, 0, dim)
+    shape = blocks.shape
+    return blocks.reshape(*shape[:dim], shape[dim] * shape[dim + 1], *shape[dim + 2 :])
+
+
+def exchange_in_pairs(x, axis, split_dim, concat_dim):
+    length, index = (lax.axis_size(axis), lax.axis_index(axis))
+    pieces = cut_along(x, split_dim, length)
+    outs = [pieces[index]]
+    for step in range(1, length):
+        sent = pieces[index ^ step]
+        outs.append(lax.ppermute(sent, axis, [(i, i ^ step) for i in range(length)]))
+    pieces = jnp.stack(outs)[index ^ jnp.arange(length)]
+    return joined_along(pieces, concat_dim)
 
 
 def local(value_in, cotangent, state_util, taste, tiles, dest_block, counts):
@@ -37,12 +59,8 @@
         request.reshape(device_count, capacity), "state", split_axis=0, concat_axis=0, tiled=True
     )
     outgoing = jnp.take(value_blocks, jnp.clip(wanted.reshape(-1), 0, block_count - 1), axis=0)
-    incoming = lax.all_to_all(
-        outgoing.reshape(device_count, capacity, tile_rows, type_width),
-        "state",
-        split_axis=0,
-        concat_axis=0,
-        tiled=True,
+    incoming = exchange_in_pairs(
+        outgoing.reshape(device_count, capacity, tile_rows, type_width), "state", 0, 0
     )
     table = jnp.concatenate(
         [value_blocks, incoming.reshape(device_count * capacity, tile_rows, type_width)], axis=0

time: 340 us -> 343 us (level)
  blocking collectives: 34 us -> 22.3 us
  starting transfers between devices: 8.47 us -> 14.4 us
  local copies, waits for them, and re-layouts: 125 us -> 130 us
    ppermute x0 -> x3, waiting for transfers between devices: none -> 61 us  [exchange_in_pairs(): lax.ppermute(sent, axis, [(i, i ^ step) for i in range(length)])]
    all_to_all x1, waiting for transfers between devices: 63.7 us -> 4.15 us  [local(): lax.all_to_all(request.reshape(device_count, capacity), 'state', split_ax...]
    all_to_all x1 -> x0, blocking collectives: 11.7 us -> none  [local(): lax.all_to_all(request.reshape(device_count, capacity), 'state', split_ax...]
    gather x0 -> x1, local copies, waits for them, and re-layouts: none -> 4.45 us  [exchange_in_pairs(): pieces = jnp.stack(outs)[index ^ jnp.arange(length)]]
    ppermute x0 -> x3, starting transfers between devices: none -> 4.39 us  [exchange_in_pairs(): lax.ppermute(sent, axis, [(i, i ^ step) for i in range(length)])]
  transfers between devices with their start and end apart: 2 -> 5, of which waited for: 1 -> 3; matrix products, arithmetic and copies ran while one was open for 27% -> 27% of each run, Pallas kernels for 0% -> 0%
where the time goes in v1:
time: 343 us; the launch traced here: 340 us
  local copies, waits for them, and re-layouts  130 us (38%)
  matrix products  67.8 us (20%)
  waiting for transfers between devices  65.2 us (19%)
  other arithmetic  39.9 us (12%)
  blocking collectives  22.3 us (7%)
  starting transfers between devices  14.4 us (4%)
    ppermute x3, waiting for transfers between devices, exchange_in_pairs(): lax.ppermute(sent, axis, [(i, i ^ step) for i in range(length)])  61 us
    reshape x1, local copies, waits for them, and re-layouts, local(): contrib = jnp.einsum('bamij,baik->bamjk', tiles, scaled, preferred_elemen...  49.2 us
    gather x2, local copies, waits for them, and re-layouts, local(): picked = jnp.take(table, lookup, axis=0)  46.1 us
    dot_general x1, matrix products, local(): jnp.einsum('bamij,baik->bamjk', tiles, scaled, preferred_element_type=jnp...  24.5 us
    dot_general x1, matrix products, local(): jnp.einsum('rd,rjk->djk', local_select, contrib, precision=lax.Precision....  23.2 us
    dot_general x1, matrix products, local(): jnp.einsum('bamij,bamjk->baik', tiles, picked, preferred_element_type=jnp...  15 us
    psum x1, blocking collectives, local(): lax.psum(jnp.sum(grad_q, axis=(0, 2)), 'state')  12.2 us
    psum x1, blocking collectives, local(): lax.psum(util_part, 'type') / (type_width * lax.axis_size('type'))  10.1 us
  transfers between devices with their start and end apart: 5, of which 3 were waited for; matrix products, arithmetic and copies ran while one was open for 27% of the time, Pallas kernels for 0%

profile of v1, /device:TPU:0, one launch (start us, length us, event | category | flops | bytes accessed | tf_op | source)
XLA Modules:
  0.0 340.4 jit_solution(16940988382889361916)
XLA Ops:
  0.6 0.8 copy.37
  1.4 0.1 iota_compare_fusion.1
  1.5 0.1 lt.128
  1.6 0.1 lt.131
  1.7 0.8 copy.38
  2.5 0.1 reshape.415
  2.6 0.1 reshape.419
  2.8 1.2 reduce-window.6
  4.0 0.1 slice.20
  4.1 0.1 copy.43
  4.3 0.1 copy.44
  4.4 0.1 add_bitcast_fusion
  4.5 1.2 scatter_custom_fusion
  5.7 0.7 all_to_all.9
  6.4 6.3 %all-to-all-start = ((s32[4,1,6]{2,1,0:T(1,128)}), s32[4,1,6]{2,1,0:T(1,128)S(1)}, u32[]{:S(2)}, u32[]{:S(2)}) async-start(s32[4,1,6]{2,1,0:T(1,128)} %bitcast.7), calls=%async_computation | async-start | bytes 4096 | tf_op jit(solution)/shard_map/all_to_all | solution.py:58
  12.7 0.1 reduce_sum.41
  12.8 1.2 scatter_custom_fusion.1
  14.1 4.1 %all-to-all-done = s32[4,1,6]{2,1,0:T(1,128)S(1)} async-done(((s32[4,1,6]{2,1,0:T(1,128)}), s32[4,1,6]{2,1,0:T(1,128)S(1)}, u32[]{:S(2)}, u32[]{:S(2)}) %all-to-all-start) | async-done | bytes 128 | tf_op jit(solution)/shard_map/all_to_all | solution.py:58
  18.2 0.5 broadcast.565
  18.7 0.7 fusion.48
  19.4 0.1 min.24
  19.5 2.3 gather_fusion
  21.9 0.4 broadcast_select_fusion
  22.2 0.0 copy-start.2
  22.2 1.5 constant_dynamic-slice_fusion
  23.7 0.6 collective-permute-start.2
  24.3 1.5 collective-permute-start.1
  25.8 2.4 collective-permute-start
  28.1 0.1 broadcast_in_dim.92
  28.2 0.1 broadcast_in_dim.90
  28.3 0.0 copy-done.2
  28.3 3.0 copy.49
  31.3 0.1 compare_and_fusion
  31.4 14.9 %collective-permute-done.2 = bf16[1,6,128,512]{3,2,1,0:T(8,128)(2,1)} collective-permute-done((bf16[1,6,128,512]{3,2,1,0:T(8,128)(2,1)}, bf16[1,6,128,512]{3,2,1,0:T(8,128)(2,1)}, u32[]{:S(2)}, u32[]{:S(2)}) %collective-permute-start.2) | collective-permute-done | bytes 786464 | tf_op jit(solution)/shard_map/ppermute | solution.py:24
  46.4 46.1 %collective-permute-done.1 = bf16[1,6,128,512]{3,2,1,0:T(8,128)(2,1)} collective-permute-done((bf16[1,6,128,512]{3,2,1,0:T(8,128)(2,1)}, bf16[1,6,128,512]{3,2,1,0:T(8,128)(2,1)}, u32[]{:S(2)}, u32[]{:S(2)}) %collective-permute-start.1) | collective-permute-done | bytes 786464 | tf_op jit(solution)/shard_map/ppermute | solution.py:24
  92.5 0.0 collective-permute-done
  92.5 3.1 maximum_bitcast_fusion
  95.6 4.4 %gather_fusion.1 = bf16[4,6,128,512]{3,2,1,0:T(8,128)(2,1)} fusion(bf16[4,6,128,512]{3,2,1,0:T(8,128)(2,1)} %maximum_bitcast_fusion, s32[1024]{0:T(1024)S(1)} %pad_clamp_fusion.2), kind=kCustom, calls=%fused_computation.1 | custom fusion | bytes 6291472 | tf_op jit(solution)/shard_map/gather | solution.py:25
  100.0 0.0 copy-done.1
  100.0 4.7 %pad_maximum_fusion = bf16[40,128,512]{2,1,0:T(8,128)(2,1)} fusion(bf16[24,128,512]{2,1,0:T(8,128)(2,1)} %bitcast.92, bf16[16,128,512]{2,1,0:T(8,128)(2,1)S(1)} %bitcast.88), kind=kLoop, calls=%fused_computation.21 | loop fusion | flops 2621440 | bytes 10485760 | tf_op jit(solution)/shard_map/concatenate | solution.py:65
  104.7 13.6 %gather_fusion.2 = bf16[192,128,512]{2,1,0:T(8,128)(2,1)} fusion(bf16[40,128,512]{2,1,0:T(8,128)(2,1)} %pad_maximum_fusion, s32[1024]{0:T(1024)S(1)} %pad_clamp_fusion.1), kind=kCustom, calls=%fused_computation.2 | custom fusion | bytes 50332416 | tf_op jit(solution)/shard_map/jit(_take)/gather | solution.py:69
  118.3 32.6 %copy.47 = bf16[16,2,6,128,512]{3,4,2,1,0:T(8,128)(2,1)} copy(bf16[16,2,6,128,512]{4,3,2,1,0:T(8,128)(2,1)} %bitcast.86) | data formatting | bytes 50331648 | tf_op jit(solution)/shard_map/jit(_take)/gather | solution.py:69
  150.9 0.0 copy-done.3
  150.9 0.0 copy-done.4
  150.9 15.0 %fusion.49 = (f32[16,128,512]{1,2,0:T(8,128)}, f32[16,2,128,512]{2,3,1,0:T(8,128)S(1)}) fusion(bf16[16,2,6,128,128]{4,3,2,1,0:T(8,128)(2,1)} %param.11, bf16[16,2,6,128,512]{3,4,2,1,0:T(8,128)(2,1)} %copy.47, pred[16,2,6]{2,1,0:T(4,128)(4,1)S(1)} %compare_and_fusion, pred[16,2,6]{2,1,0:T(4,128)(4,1)S(1)} %iota_compare_fusion.1, ...), kind=kOutput, calls=%fused_computation.111 | convolution fusion | flops 3253731328 | bytes 44061056 | tf_op jit(solution)/shard_map/bamij,bamjk->baik/dot_general | solution.py:72
  165.8 9.7 %exponential_reduce_fusion = f32[16,128,512]{1,2,0:T(8,128)} fusion(f32[16,2,128,512]{2,3,1,0:T(8,128)S(1)} %get-tuple-element.21, f32[16,128,512]{1,2,0:T(8,128)} %get-tuple-element.20), kind=kLoop, calls=%fused_computation.17 | loop fusion | flops 3145728 | bytes 16777216 | tf_op jit(solution)/shard_map/reduce_sum | solution.py:78
  175.6 6.0 %log_add_fusion = f32[16,128,512]{1,2,0:T(8,128)} fusion(f32[16,128,512]{1,2,0:T(8,128)} %get-tuple-element.20, f32[16,128,512]{1,2,0:T(8,128)} %exponential_reduce_fusion), kind=kLoop, calls=%fused_computation.27 | loop fusion | flops 1048576 | bytes 12582912 | tf_op jit(solution)/shard_map/add | solution.py:78
  181.6 24.5 %fusion.10 = f32[16,2,512,6,128]{4,2,3,1,0:T(8,128)} fusion(bf16[16,2,6,128,128]{4,3,2,1,0:T(8,128)(2,1)} %param.11, f32[16,2,128,512]{2,3,1,0:T(8,128)} %copy-done, f32[16,128,512]{1,2,0:T(8,128)} %log_add_fusion, f32[16,128,512]{1,2,0:T(8,128)} %copy.49), kind=kOutput, calls=%fused_computation.23 | convolution fusion | flops 3229614080 | bytes 73400320 | tf_op jit(solution)/shard_map/bamij,baik->bamjk/dot_general | solution.py:91
  206.1 4.4 %gather_fusion.3 = bf16[24,128,512]{1,2,0:T(8,128)(2,1)S(1)} fusion(f32[192,128,512]{1,2,0:T(8,128)} %bitcast.84, s32[1024]{0:T(1024)S(1)} %pad_clamp_fusion), kind=kCustom, calls=%fused_computation.3 | custom fusion | bytes 6291552 | tf_op jit(solution)/shard_map/jit(_take)/gather | solution.py:95
  210.6 2.8 copy.51
  213.3 5.0 %select_convert_fusion = bf16[4,6,128,512]{3,2,1,0:T(8,128)(2,1)} fusion(bf16[4,6,128,512]{3,2,1,0:T(8,128)(2,1)} %bitcast.91, pred[4,6]{1,0:T(4,128)(4,1)S(1)} %broadcast_in_dim.92, pred[4,6]{1,0:T(4,128)(4,1)S(1)} %broadcast_in_dim.90), kind=kLoop, calls=%fused_computation.18 | loop fusion | flops 3145728 | bytes 6291504 | tf_op jit(solution)/shard_map/convert_element_type | solution.py:96
  218.3 3.7 %all-to-all-start.1 = ((bf16[4,6,128,512]{3,2,1,0:T(8,128)(2,1)}), bf16[4,6,128,512]{3,2,1,0:T(8,128)(2,1)S(1)}, u32[]{:S(2)}, u32[]{:S(2)}) async-start(bf16[4,6,128,512]{3,2,1,0:T(8,128)(2,1)} %select_convert_fusion), calls=%async_computation.1 | async-start | bytes 6291456 | tf_op jit(solution)/shard_map/all_to_all | solution.py:97
  222.0 0.1 reshape.421
  222.1 5.3 %copy.48 = f32[16,128,512]{2,1,0:T(8,128)} copy(f32[16,128,512]{1,2,0:T(8,128)} %log_add_fusion) | data formatting | bytes 8388608 | tf_op jit(solution)/shard_map/add | solution.py:78
  227.4 49.2 %copy.50 = f32[192,128,512]{2,0,1:T(8,128)} copy(f32[192,128,512]{1,2,0:T(8,128)} %bitcast.85) | data formatting | bytes 100663296 | tf_op jit(solution)/shard_map/reshape | solution.py:93
  276.6 7.5 %fusion.7 = (f32[2,512]{1,0:T(2,128)S(1)}, f32[16,2,128]{2,1,0:T(2,128)S(1)}) fusion(f32[16,2,128,512]{2,3,1,0:T(8,128)} %copy-done, f32[16,128,512]{1,2,0:T(8,128)} %log_add_fusion, f32[16,128,512]{1,2,0:T(8,128)} %copy.49), kind=kLoop, calls=%fused_computation.19 | loop fusion | flops 8383488 | bytes 16797696 | tf_op jit(solution)/shard_map/reduce_sum | solution.py:85
  284.1 12.2 %psum.15 = f32[2,512]{1,0:T(2,128)S(1)} all-reduce(f32[2,512]{1,0:T(2,128)S(1)} %get-tuple-element.4), channel_id=1, replica_groups=mesh['groups'=2,'state'=4,'type'=4] {'state'}, use_global_device_ids=true, to_apply=%region_10.11 | all-reduce | flops 1024 | bytes 8192 | tf_op jit(solution)/shard_map/psum | solution.py:85
  296.3 10.1 %psum.14 = f32[2,2048]{1,0:T(2,128)S(1)} all-reduce(f32[2,2048]{1,0:T(2,128)S(1)} %bitcast.96), channel_id=1, replica_groups=mesh['groups'=2,'state'=4,'type'=4] {'type'}, use_global_device_ids=true, to_apply=%region_8.9 | all-reduce | flops 4096 | bytes 32768 | tf_op jit(solution)/shard_map/psum | solution.py:84
  306.4 0.6 broadcast_multiply_fusion.1
  307.0 0.6 broadcast_multiply_fusion
  307.6 23.2 %fusion.26 = f32[16,128,512]{2,0,1:T(8,128)} fusion(f32[192,128,512]{2,0,1:T(8,128)} %copy.50, s32[192]{0:T(256)S(1)} %and_select_fusion.4, pred[192]{0:T(512)(128)(4,1)S(1)} %get-tuple-element.10), kind=kOutput, calls=%fused_computation.50 | convolution fusion | flops 2415925248 | bytes 54526912 | tf_op jit(solution)/shard_map/rd,rjk->djk/dot_general | solution.py:108
  330.9 0.0 all-to-all-done.1
  330.9 5.1 %fusion.20 = f32[16,128,512]{2,0,1:T(8,128)S(1)} fusion(f32[16,128,512]{2,0,1:T(8,128)} %fusion.26, s32[24]{0:T(128)S(1)} %reshape.421, bf16[3,8,128,512]{3,2,1,0:T(8,128)(2,1)S(1)} %bitcast.90), kind=kOutput, calls=%fused_computation.33 | convolution fusion | flops 51380608 | bytes 11534432 | tf_op jit(solution)/shard_map/dot_general | solution.py:110
  335.9 4.4 %copy.53 = f32[16,128,512]{2,1,0:T(8,128)} copy(f32[16,128,512]{2,0,1:T(8,128)S(1)} %fusion.20) | data formatting | bytes 8388608 | tf_op jit(solution)/shard_map/add | solution.py:115
  (26 shorter events, 0.2 us)
Async XLA Ops:
  6.4 11.8 %all-to-all-start = ((s32[4,1,6]{2,1,0:T(1,128)}), s32[4,1,6]{2,1,0:T(1,128)S(1)}, u32[]{:S(2)}, u32[]{:S(2)}) async-start(s32[4,1,6]{2,1,0:T(1,128)} %bitcast.7), calls=%async_computation | async-start | bytes 4096 | tf_op jit(solution)/shard_map/all_to_all | solution.py:58
  22.2 6.1 %copy-start.2 = (bf16[2048,512]{1,0:T(8,128)(2,1)S(1)}, bf16[2048,512]{1,0:T(8,128)(2,1)}, u32[]{:S(2)}) copy-start(bf16[2048,512]{1,0:T(8,128)(2,1)} %param.8) | copy-start | bytes 6291460
  23.7 22.6 %collective-permute-start.2 = (bf16[1,6,128,512]{3,2,1,0:T(8,128)(2,1)}, bf16[1,6,128,512]{3,2,1,0:T(8,128)(2,1)}, u32[]{:S(2)}, u32[]{:S(2)}) collective-permute-start(bf16[1,6,128,512]{3,2,1,0:T(8,128)(2,1)} %get-tuple-element.15), channel_id=1, source_target_pairs={{0,12},{4,8},{8,4},{12,0},{1,13},{5,9},{9,5},{13,1},{2,14},{6,10},... | collective-permute-start | bytes 2359304 | tf_op jit(solution)/shard_map/ppermute | solution.py:24
  24.3 68.2 %collective-permute-start.1 = (bf16[1,6,128,512]{3,2,1,0:T(8,128)(2,1)}, bf16[1,6,128,512]{3,2,1,0:T(8,128)(2,1)}, u32[]{:S(2)}, u32[]{:S(2)}) collective-permute-start(bf16[1,6,128,512]{3,2,1,0:T(8,128)(2,1)} %get-tuple-element.16), channel_id=1, source_target_pairs={{0,8},{4,12},{8,0},{12,4},{1,9},{5,13},{9,1},{13,5},{2,10},{6,14},... | collective-permute-start | bytes 2359304 | tf_op jit(solution)/shard_map/ppermute | solution.py:24
  25.8 66.7 %collective-permute-start = (bf16[1,6,128,512]{3,2,1,0:T(8,128)(2,1)}, bf16[1,6,128,512]{3,2,1,0:T(8,128)(2,1)}, u32[]{:S(2)}, u32[]{:S(2)}) collective-permute-start(bf16[1,6,128,512]{3,2,1,0:T(8,128)(2,1)} %get-tuple-element.17), channel_id=1, source_target_pairs={{0,4},{4,0},{8,12},{12,8},{1,5},{5,1},{9,13},{13,9},{2,6},{6,2},{1... | collective-permute-start | bytes 2359304 | tf_op jit(solution)/shard_map/ppermute | solution.py:24
  95.6 4.5 %copy-start.1 = (bf16[2048,512]{1,0:T(8,128)(2,1)S(1)}, bf16[2048,512]{1,0:T(8,128)(2,1)}, u32[]{:S(2)}) copy-start(bf16[2048,512]{1,0:T(8,128)(2,1)} %param.7) | copy-start | bytes 6291460
  118.3 32.6 %copy-start.3 = (f32[2,2048]{1,0:T(2,128)S(1)}, f32[2,2048]{1,0:T(2,128)}, u32[]{:S(2)}) copy-start(f32[2,2048]{1,0:T(2,128)} %param.9) | copy-start | bytes 49156
  118.3 32.6 %copy-start.4 = (f32[2,512]{1,0:T(2,128)S(1)}, f32[2,512]{1,0:T(2,128)}, u32[]{:S(2)}) copy-start(f32[2,512]{1,0:T(2,128)} %param.10) | copy-start | bytes 12292
  165.8 9.7 %copy-start = (f32[16,2,128,512]{2,3,1,0:T(8,128)}, f32[16,2,128,512]{2,3,1,0:T(8,128)S(1)}, u32[]{:S(2)}) copy-start(f32[16,2,128,512]{2,3,1,0:T(8,128)S(1)} %get-tuple-element.21) | copy-start | bytes 25165828
  218.3 112.5 %all-to-all-start.1 = ((bf16[4,6,128,512]{3,2,1,0:T(8,128)(2,1)}), bf16[4,6,128,512]{3,2,1,0:T(8,128)(2,1)S(1)}, u32[]{:S(2)}, u32[]{:S(2)}) async-start(bf16[4,6,128,512]{3,2,1,0:T(8,128)(2,1)} %select_convert_fusion), calls=%async_computation.1 | async-start | bytes 6291456 | tf_op jit(solution)/shard_map/all_to_all | solution.py:97
